TPU v7x, 512 devices: a whole 4x4x16 slice. The times are simulated.
512 devices in a mesh: occ: 64 (over y, z), vir: 8 (over x, core).
Axes of the slice: x: 4, y: 4, z: 16, core: 2. Of those that a mesh axis runs over, the one named last changes fastest.
Arguments:
- t2_tiles: bfloat16 [16384, 128, 128], P(('occ', 'vir')), may hold values from -6 to 6
- tile_owner: int32 [16384, 1], P(('occ', 'vir')), may hold values from 0 to 63; in each aligned block of 32 rows (0 to 31, 32 to 63, ...) at most 2 rows name the same one
- tile_block: int32 [16384], P(('occ', 'vir')), may hold values from 0 to 1
- tile_cd: int32 [16384], P(('occ', 'vir')), may hold values from 0 to 3
- ladder_ints: bfloat16 [4096, 2048], P('vir', 'occ'), may hold values from -0.75 to 0.75
- cycle_amps: bfloat16 [16384, 1024], P('occ', 'vir'), may hold values from -6 to 6
- cycle_ints: bfloat16 [1024, 2048], P('vir'), may hold values from -0.25 to 0.25
Outputs:
- residual: bfloat16 [16384, 2048], P('occ', 'vir')
Inputs may be any that keep to these rules, and one draw needn't show every extreme that they name: `tile_owner`: among the tiles of one device (aligned blocks of 32 tiles), no owner is named more than 2 times, a bound that some block reaches.
All inputs are finite; a program needn't handle non-finite values.
Results may differ from a plain program's by a relative error of at most 0.0048.
Values may be sent and summed in bfloat16 or wider, within the bound.
A program may use at most 64 MiB of HBM per device.

v0:
```python
import jax
import jax.numpy as jnp
from jax import lax
from jax.sharding import PartitionSpec as P

NY = 4


def body(t2_tiles, tile_owner, tile_block, tile_cd, ladder_ints, cycle_amps, cycle_ints):
    n_occ = lax.axis_size("occ")
    nz = n_occ // NY
    tile_count, tile_size = t2_tiles.shape[:2]
    pair_rows = cycle_amps.shape[0]
    blocks = pair_rows // tile_size
    cd_tiles = ladder_ints.shape[0] // tile_size
    combos = blocks * cd_tiles
    y_groups = [[y * nz + z for y in range(NY)] for z in range(nz)]
    z_groups = [[y * nz + z for z in range(nz)] for y in range(NY)]
    codes = tile_owner[:, 0] * combos + tile_block * cd_tiles + tile_cd
    got_tiles = lax.all_gather(
        t2_tiles.reshape(tile_count, tile_size * tile_size),
        "occ", axis=0, tiled=True, axis_index_groups=y_groups,
    )
    got_codes = lax.all_gather(codes, "occ", axis=0, tiled=True, axis_index_groups=y_groups)
    full_ladder = lax.all_gather(ladder_ints, "occ", axis=1, tiled=True)
    my_y = lax.axis_index("occ") // nz
    targets = my_y * (nz * combos) + jnp.arange(nz * combos, dtype=jnp.int32)
    select = (got_codes[:, None] == targets[None, :]).astype(jnp.bfloat16)
    summed = jnp.einsum("sc,sx->cx", select, got_tiles, preferred_element_type=jnp.float32)
    summed = lax.psum_scatter(
        summed.astype(jnp.bfloat16), "occ", scatter_dimension=0, tiled=True,
        axis_index_groups=z_groups,
    )
    amplitudes = (
        summed.reshape(blocks, cd_tiles, tile_size, tile_size)
        .transpose(0, 2, 1, 3)
        .reshape(pair_rows, cd_tiles * tile_size)
    )
    cycle_part = jnp.dot(cycle_amps, cycle_ints, preferred_element_type=jnp.float32)
    ladder = jnp.dot(amplitudes, full_ladder, preferred_element_type=jnp.float32)
    combined = ladder + cycle_part
    return lax.psum_scatter(combined, "vir", scatter_dimension=1, tiled=True).astype(jnp.bfloat16)


def solution(mesh):
    in_specs = (
        P(("occ", "vir"), None, None),
        P(("occ", "vir"), None),
        P(("occ", "vir")),
        P(("occ", "vir")),
        P("vir", "occ"),
        P("occ", "vir"),
        P("vir", None),
    )
    return jax.shard_map(
        body, mesh=mesh, in_specs=in_specs, out_specs=P("occ", "vir"), check_vma=False
    )
```

profile of v0, /device:TPU:8, one launch (start us, length us, event | category | flops | bytes accessed | tf_op | source)
XLA Modules:
  0.0 276.3 jit_solution(14078321033203667457)
XLA Ops:
  7.4 0.0 copy-start
  7.4 0.0 copy-start.2
  7.4 0.0 copy-start.4
  7.4 0.0 copy-start.3
  7.4 0.0 all-gather.3.cloned.1.call-start
  7.4 2.9 %copy.17 = bf16[4,8,128,128]{3,1,2,0:T(8,128)(2,1)} copy(bf16[4,8,128,128]{3,2,1,0:T(8,128)(2,1)} %bitcast.26) | data formatting | bytes 2097152
  10.3 0.0 all-gather.3.cloned.1.call-update
  10.4 0.0 reduce-scatter.3.cloned.1.call-start
  10.4 1.3 dynamic-slice
  12.4 0.0 copy-done.2
  12.4 0.0 copy-done.4
  12.4 0.0 copy-done.3
  12.4 0.1 fusion.6
  12.5 9.4 %all-reduce = s32[128]{0:T(128)S(1)} all-reduce(s32[128]{0:T(128)S(1)} %fusion.6), channel_id=1, replica_groups={{0,128,256,384},{8,136,264,392},{16,144,272,400},{24,152,280,408},{32,1..., use_global_device_ids=true, to_apply=%add | all-reduce | flops 128 | bytes 1024
  21.9 48.3 %all-gather.3.cloned.1.call-done = bf16[128,16384]{1,0:T(8,128)(2,1)} async-done(((bf16[32,16384]{1,0:T(8,128)(2,1)}), bf16[128,16384]{1,0:T(8,128)(2,1)}) %all-gather.3.cloned.1.call-update) | async-done | bytes 4194320 | tf_op jit(solution)/shard_map/all_gather | solution.py:20
  70.2 5.5 %convolution_convert_fusion = bf16[128,16384]{1,0:T(8,128)(2,1)} fusion(bf16[128,16384]{1,0:T(8,128)(2,1)} %all-gather.3.cloned.1.call-done, s32[128]{0:T(128)S(1)} %iota_add_fusion, s32[128]{0:T(128)S(1)} %all-reduce), kind=kOutput, calls=%fused_computation | convolution fusion | flops 538984448 | bytes 8389632 | tf_op jit(solution)/shard_map/sc,sx->cx/dot_general | solution.py:29
  75.7 0.0 copy-start.1
  75.7 0.0 reduce-scatter.3.cloned.1.call-update
  75.7 0.0 all-gather.5.cloned.1.call-start
  75.8 0.5 all-gather.5.cloned.1.call-update
  76.3 0.0 reduce-scatter.5.cloned.1.call-start
  76.4 0.0 copy-done
  76.4 0.2 copy-done.1
  76.5 0.4 fusion.7
  77.0 79.8 %reduce-scatter.3.cloned.1.call-done = bf16[8,16384]{1,0:T(8,128)(2,1)} async-done(((bf16[128,16384]{1,0:T(8,128)(2,1)}), bf16[8,16384]{1,0:T(8,128)(2,1)}) %reduce-scatter.3.cloned.1.call-update) | async-done | bytes 262160 | tf_op jit(solution)/shard_map/reduce_scatter | solution.py:30
  156.7 1.0 copy.10
  157.7 0.2 copy.8
  157.9 67.5 %all-gather.5.cloned.1.call-done = bf16[512,2048]{0,1:T(8,128)(2,1)} async-done(((bf16[512,32]{0,1:T(8,128)(2,1)}), bf16[512,2048]{0,1:T(8,128)(2,1)}) %all-gather.5.cloned.1.call-update) | async-done | bytes 2097168 | tf_op jit(solution)/shard_map/all_gather | solution.py:25
  225.4 3.7 %convolution_add_fusion = f32[256,2048]{1,0:T(8,128)} fusion(f32[256,2048]{1,0:T(8,128)S(1)} %fusion.7, bf16[512,2048]{0,1:T(8,128)(2,1)} %all-gather.5.cloned.1.call-done, bf16[32,8,4,128]{3,2,1,0:T(4,128)(2,1)S(1)} %bitcast.25), kind=kOutput, calls=%fused_computation.1 | convolution fusion | flops 537395200 | bytes 6553600 | tf_op jit(solution)/shard_map/dot_general | solution.py:40
  229.1 0.0 reduce-scatter.5.cloned.1.call-update
  229.1 38.2 %reduce-scatter.5.cloned.1.call-done = f32[256,256]{1,0:T(8,128)} async-done(((f32[256,2048]{1,0:T(8,128)}), f32[256,256]{1,0:T(8,128)}) %reduce-scatter.5.cloned.1.call-update) | async-done | bytes 262160 | tf_op jit(solution)/shard_map/reduce_scatter | solution.py:42
  267.3 1.6 convert_element_type.8
  (2 shorter events, 0.0 us)
Async XLA Ops:
  7.4 69.0 %copy-start = (bf16[128,2048]{1,0:T(8,128)(2,1)S(1)}, bf16[128,2048]{1,0:T(8,128)(2,1)}, u32[]{:S(2)}) copy-start(bf16[128,2048]{1,0:T(8,128)(2,1)} %param.13) | copy-start | bytes 1572868
  7.4 5.0 %copy-start.2 = (s32[32]{0:T(128)S(1)}, s32[32]{0:T(128)}, u32[]{:S(2)}) copy-start(s32[32]{0:T(128)} %param.10) | copy-start | bytes 388
  7.4 5.0 %copy-start.4 = (s32[32,1]{0,1:T(1,128)S(1)}, s32[32,1]{0,1:T(1,128)}, u32[]{:S(2)}) copy-start(s32[32,1]{0,1:T(1,128)} %param.8) | copy-start | bytes 388
  7.4 5.0 %copy-start.3 = (s32[32]{0:T(128)S(1)}, s32[32]{0:T(128)}, u32[]{:S(2)}) copy-start(s32[32]{0:T(128)} %param.9) | copy-start | bytes 388
  7.4 62.8 %all-gather.3.cloned.1.call-start = ((), (), s32[]{:S(2)}) async-start(), calls=%async_computation.2 | async-start | bytes 5242880 | tf_op jit(solution)/shard_map/all_gather | solution.py:20
  10.4 146.4 %reduce-scatter.3.cloned.1.call-start = ((), (), s32[]{:S(2)}) async-start(), calls=%async_computation.3 | async-start | bytes 4456448 | tf_op jit(solution)/shard_map/reduce_scatter | solution.py:30
  75.7 0.8 copy-start.1
  75.7 149.7 %all-gather.5.cloned.1.call-start = ((), (), s32[]{:S(2)}) async-start(), calls=%async_computation.4 | async-start | bytes 2129920 | tf_op jit(solution)/shard_map/all_gather | solution.py:25
  76.3 191.0 %reduce-scatter.5.cloned.1.call-start = ((), (), s32[]{:S(2)}) async-start(), calls=%async_computation.5 | async-start | bytes 2359296 | tf_op jit(solution)/shard_map/reduce_scatter | solution.py:42
Sparse Core Ops, SparseCore 0:
  10.5 59.6 all-gather.2
  75.8 80.8 reduce-scatter.2
Sparse Core Ops, SparseCore 1:
  79.1 146.2 all-gather.4
  229.2 38.0 reduce-scatter.4
where the time goes:
time: 277 us; the launch traced here: 276 us
  waiting for transfers between devices  234 us (84%)
  between operations  15.6 us (6%)
  matrix products  9.58 us (3%)
  blocking collectives  9.41 us (3%)
  local copies, waits for them, and re-layouts  5.58 us (2%)
    reduce_scatter x1, waiting for transfers between devices, body(): lax.psum_scatter(summed.astype(jnp.bfloat16), 'occ', scatter_dimension=0,...  79.8 us
    all_gather x1, waiting for transfers between devices, body(): full_ladder = lax.all_gather(ladder_ints, 'occ', axis=1, tiled=True)  67.5 us
    all_gather x1, waiting for transfers between devices, body(): lax.all_gather(t2_tiles.reshape(tile_count, tile_size * tile_size), 'occ'...  48.3 us
    reduce_scatter x1, waiting for transfers between devices, body(): lax.psum_scatter(combined, 'vir', scatter_dimension=1, tiled=True)  38.2 us
    unnamed x1, blocking collectives  9.41 us
  transfers between devices with their start and end apart: 4, of which 4 were waited for; matrix products, arithmetic and copies ran while one was open for 1% of the time, Pallas kernels for 0%

commit v1 on v0

v1 whole, which is shorter than its diff:
```python
import functools

import jax
import jax.numpy as jnp
from jax import lax
from jax.experimental import pallas as pl
from jax.experimental.pallas import tpu as pltpu
from jax.sharding import PartitionSpec as P

MESH = pl.DeviceIdType.MESH
NY = 4
NC = 4
LAG = 2
BF = jnp.bfloat16
F32 = jnp.float32


def kernel(
    t2_ref, code_ref, lad_ref, camp_ref, cint_ref, out_ref,
    gath, codes, sel, ysum, zin, lgat, part, acc, amps, pout, pin, xs, xh, xi,
    ysend, yrecv, csend, crecv, zsend, zrecv, lzs, lzr, lys, lyr, ps, pr, xsend, xrecv, local,
):
    nz = lgat.shape[1]
    rows = t2_ref.shape[0]
    cr = rows // NC
    half = cr // 2
    nx = pout.shape[0]
    occ, vir = lax.axis_index("occ"), lax.axis_index("vir")
    y, z = occ // nz, occ % nz
    x, core = vir // 2, vir % 2

    def at_y(d):
        return (y + d + NY) % NY

    def at_z(d):
        return (z + d + nz) % nz

    def at_x(d):
        return (x + d + nx) % nx

    def to_y(d):
        return {"occ": at_y(d) * nz + z}

    def to_z(d):
        return {"occ": y * nz + at_z(d)}

    def to_x(d):
        return {"vir": at_x(d) * 2 + core}

    partner = {"vir": x * 2 + (1 - core)}

    def remote(src, dst, send, recv, where):
        return pltpu.make_async_remote_copy(
            src_ref=src, dst_ref=dst, send_sem=send, recv_sem=recv, device_id=where,
            device_id_type=MESH,
        )

    def chunk(c):
        return pl.ds(c * cr, cr)

    def own_y(c, d):
        return remote(
            t2_ref.at[chunk(c)], gath.at[chunk(c), y], ysend.at[c, d], yrecv.at[c, d],
            to_y(1 - 2 * d),
        )

    def own_y_in(c, d):
        return remote(
            t2_ref.at[chunk(c)], gath.at[chunk(c), at_y(2 * d - 1)], ysend.at[c, d],
            yrecv.at[c, d], to_y(1 - 2 * d),
        )

    def piece(c, d):
        return pl.ds(c * cr + d * half, half)

    def fwd_y(c, d):
        block = gath.at[piece(c, d), at_y(2 * d - 1)]
        return remote(block, block, ysend.at[c, 2 + d], yrecv.at[c, 2 + d], to_y(1 - 2 * d))

    def fwd_y_in(c, d):
        block = gath.at[piece(c, d), at_y(2)]
        return remote(block, block, ysend.at[c, 2 + d], yrecv.at[c, 2 + d], to_y(1 - 2 * d))

    def code_out(d):
        return remote(code_ref, codes.at[y], csend.at[d - 1], crecv.at[d - 1], to_y(d))

    def code_in(d):
        return remote(code_ref, codes.at[at_y(-d)], csend.at[d - 1], crecv.at[d - 1], to_y(d))

    def arm(c, d):
        return nz // 2 if (c + d) % 2 == 0 else nz - 1 - nz // 2

    def z_copy(c, d, s):
        block = ysum.at[at_z((1 - 2 * d) * (arm(c, d) - s)), chunk(c)]
        return remote(
            block, zin.at[d, s, chunk(c)], zsend.at[c, d, s], zrecv.at[c, d, s], to_z(1 - 2 * d)
        )

    steps = (nz // 2, nz - 1 - nz // 2)

    def lad_z(d, s):
        block = lgat.at[y, at_z((2 * d - 1) * s)]
        src = lad_ref if s == 0 else block
        return remote(src, block, lzs.at[d, s], lzr.at[d, s], to_z(1 - 2 * d))

    def lad_z_in(d, s):
        block = lgat.at[y, at_z((2 * d - 1) * (s + 1))]
        return remote(block, block, lzs.at[d, s], lzr.at[d, s], to_z(1 - 2 * d))

    def lad_y(d, source):
        block = lgat.at[at_y(source)]
        return remote(block, block, lys.at[d], lyr.at[d], to_y(1 - 2 * d))

    def lad_fwd(d, source):
        block = lgat.at[at_y(source), pl.ds(d * (nz // 2), nz // 2)]
        return remote(block, block, lys.at[2 + d], lyr.at[2 + d], to_y(1 - 2 * d))

    barrier = pltpu.get_barrier_semaphore()
    peers = [to_y(1), to_y(2), to_y(-1), to_z(1), to_z(-1), to_x(1), to_x(-1), partner]
    for peer in peers:
        pl.semaphore_signal(barrier, inc=1, device_id=peer, device_id_type=MESH)
    pl.semaphore_wait(barrier, len(peers))

    for d in (1, 2, 3):
        code_out(d).start()
    for c in (0, 1):
        for d in (0, 1):
            own_y(c, d).start()
    mine_t2 = pltpu.make_async_copy(t2_ref, gath.at[:, y], local.at[0])
    mine_lad = pltpu.make_async_copy(lad_ref, lgat.at[y, z], local.at[1])
    mine_t2.start()
    mine_lad.start()

    def stage_a(c):
        for d in (0, 1):
            own_y_in(c, d).wait_recv()
            fwd_y(c, d).start()
        if c + 2 < NC:
            for d in (0, 1):
                own_y(c + 2, d).start()

    def lad_step(s):
        for d in (0, 1):
            if 1 <= s <= steps[d]:
                lad_z_in(d, s - 1).wait_recv()
            if s < steps[d]:
                lad_z(d, s).start()

    lad_step(0)

    @pl.loop(0, part.shape[0])
    def _(j):
        part[j] = jnp.dot(camp_ref[...], cint_ref[j], preferred_element_type=F32)

    for s in (1, 2):
        lad_step(s)
    stage_a(0)
    for s in range(3, steps[0] + 1):
        lad_step(s)
    mine_t2.wait()
    mine_lad.wait()

    codes[y] = code_ref[...]
    for d in (1, 2, 3):
        code_in(d).wait_recv()
    per_y = t2_ref.shape[1]
    lanes = code_ref.shape[1]
    dests = sel.shape[0]
    want = (lax.broadcasted_iota(jnp.int32, (dests, lanes), 0) + y * dests).astype(F32)
    lane = lax.broadcasted_iota(jnp.int32, (1, lanes), 1)
    for h in range(NY * per_y // lanes):
        row = jnp.where(lane < per_y, codes[2 * h, 0:1], codes[2 * h + 1, 0:1])
        sel[:, h * lanes:(h + 1) * lanes] = jnp.where(want == row, 1.0, 0.0).astype(BF)

    def stage_b(c):
        for d in (0, 1):
            fwd_y_in(c, d).wait_recv()

        @pl.loop(0, cr // 4)
        def _(i):
            for u in range(4):
                r = c * cr + i * 4 + u
                tiles = gath[r].reshape(NY * per_y, gath.shape[3])
                got = jnp.dot(sel[...], tiles, preferred_element_type=F32)
                ysum[:, r] = got.astype(BF).reshape(nz, dests // nz, gath.shape[3])

        for d in (0, 1):
            z_copy(c, d, 0).start()

    def z_step(c, s):
        for d in (0, 1):

            @pl.when(s < arm(c, d))
            def _():
                z_copy(c, d, s - 1).wait_recv()
                dest = at_z((1 - 2 * d) * (arm(c, d) - s))
                ysum[dest, chunk(c)] = ysum[dest, chunk(c)] + zin[d, s - 1, chunk(c)]
                z_copy(c, d, s).start()

    def z_last(c):
        total = ysum[z, chunk(c)].astype(F32)
        for d in (0, 1):
            z_copy(c, d, arm(c, d) - 1).wait_recv()
            total = total + zin[d, arm(c, d) - 1, chunk(c)].astype(F32)
        depth = acc.shape[0] // NC
        acc[pl.ds(c * depth, depth)] = total.reshape(depth, acc.shape[1])

    last = nz // 2

    @pl.loop(0, LAG * (NC - 1) + last + 1)
    def _(tick):
        for c in range(NC):
            s = tick - LAG * c
            if c > 0:

                @pl.when(s == -1)
                def _():
                    stage_a(c)
                    if c == NC - 1:
                        for d in (0, 1):
                            lad_y(d, 0).start()

            @pl.when(s == 0)
            def _():
                stage_b(c)

            @pl.when((s > 0) & (s < last))
            def _():
                z_step(c, s)

            @pl.when(s == last)
            def _():
                z_last(c)

            if c == NC - 1:

                @pl.when(s == 3)
                def _():
                    for d in (0, 1):
                        lad_y(d, 2 * d - 1).wait_recv()
                        lad_fwd(d, 2 * d - 1).start()

    for d in (0, 1):
        lad_fwd(d, 2).wait_recv()

    per_owner = ysum.shape[2]
    cds = amps.shape[1] // acc.shape[1]
    blocks = per_owner // (2 * cds)
    for b in range(blocks):
        for h in range(2):
            for cd in range(cds):
                start = (b * cds + cd) * 2 + h
                first = (b * 2 + h) * rows
                amps[first:first + rows, cd * acc.shape[1]:(cd + 1) * acc.shape[1]] = acc[
                    pl.ds(start, rows, stride=per_owner), :
                ].astype(BF)

    def block_of(j):
        per = lgat.shape[0] * nz // (2 * nx)
        first = j * per
        piece_l = lgat[first // nz, pl.ds(first % nz, per)]
        piece_l = piece_l.reshape(per * lgat.shape[2], lgat.shape[3])
        return part[j] + lax.dot_general(
            amps[...], piece_l, (((1,), (1,)), ((), ())), preferred_element_type=F32
        )

    def pair(i):
        return remote(pout.at[i], pin.at[i], ps.at[i], pr.at[i], partner)

    order = (2, 1, 3, 0)
    for n in order:
        i = at_x(n)
        pout[i] = block_of(i * 2 + (1 - core)).astype(BF)
        pair(i).start()
    for n in order:
        i = at_x(n)
        part[i * 2 + core] = block_of(i * 2 + core)

    mid = xs.shape[1] // 2

    def summed(n):
        i = at_x(n)
        pair(i).wait_recv()
        return part[i * 2 + core] + pin[i].astype(F32)

    def far(d):
        return remote(
            xs.at[2, pl.ds(d * mid, mid)], xh.at[d], xsend.at[d], xrecv.at[d], to_x(1 - 2 * d)
        )

    def near(d):
        return remote(xs.at[d], xi.at[d], xsend.at[2 + d], xrecv.at[2 + d], to_x(1 - 2 * d))

    xs[2] = summed(2).astype(BF)
    for d in (0, 1):
        far(d).start()
    for d in (0, 1):
        part[at_x(1 - 2 * d) * 2 + core] = summed(1 - 2 * d)
    part[x * 2 + core] = summed(0)
    for d in (0, 1):
        far(d).wait_recv()
        j = at_x(1 - 2 * d) * 2 + core
        both = part[j, pl.ds(d * mid, mid)] + xh[d].astype(F32)
        xs[d, pl.ds(d * mid, mid)] = both.astype(BF)
        xs[d, pl.ds((1 - d) * mid, mid)] = part[j, pl.ds((1 - d) * mid, mid)].astype(BF)
        near(d).start()
    for d in (0, 1):
        near(d).wait_recv()
    out_ref[...] = (part[x * 2 + core] + xi[0].astype(F32) + xi[1].astype(F32)).astype(BF)

    for d in (1, 2, 3):
        code_out(d).wait_send()
    for c in range(NC):
        for d in (0, 1):
            own_y(c, d).wait_send()
            fwd_y(c, d).wait_send()
            for s in range(arm(c, d)):
                z_copy(c, d, s).wait_send()
    for d in (0, 1):
        for s in range(steps[d]):
            lad_z(d, s).wait_send()
        lad_y(d, 0).wait_send()
        lad_fwd(d, 2 * d - 1).wait_send()
        far(d).wait_send()
        near(d).wait_send()
    for n in order:
        pair(at_x(n)).wait_send()


def body(n_occ, n_vir, t2_tiles, tile_owner, tile_block, tile_cd, ladder_ints, cycle_amps, cycle_ints):
    nz, nx = n_occ // NY, n_vir // 2
    count, size = t2_tiles.shape[:2]
    pair_rows, _ = cycle_amps.shape
    depth, cols = ladder_ints.shape
    ranks, all_cols = cycle_ints.shape
    blocks, cds = pair_rows // size, depth // size
    combos = blocks * cds
    rows = size // 2
    width = all_cols // n_vir
    per_y, per_owner = count * 2, combos * 2
    tiles = t2_tiles.reshape(count, 2, rows, size).transpose(2, 0, 1, 3).reshape(rows, per_y, size)
    code = tile_owner[:, 0] * combos + tile_block * cds + tile_cd
    code = (code[:, None] * 2 + jnp.arange(2, dtype=jnp.int32)[None, :]).reshape(1, per_y)
    code = jnp.tile(code, (8, 128 // per_y)).astype(F32)
    ints = cycle_ints.reshape(ranks, n_vir, width).transpose(1, 0, 2)
    vmem, dma = pltpu.VMEM, pltpu.SemaphoreType.DMA
    near = nz // 2
    return pl.pallas_call(
        kernel,
        out_shape=jax.ShapeDtypeStruct((pair_rows, width), BF),
        in_specs=[pl.BlockSpec(memory_space=vmem)] * 5,
        out_specs=pl.BlockSpec(memory_space=vmem),
        scratch_shapes=[
            vmem((rows, NY, per_y, size), BF),
            vmem((NY, 8, 128), F32),
            vmem((nz * per_owner, NY * per_y), BF),
            vmem((nz, rows, per_owner, size), BF),
            vmem((2, near, rows, per_owner, size), BF),
            vmem((NY, nz, cols, depth), BF),
            vmem((n_vir, pair_rows, width), F32),
            vmem((rows * per_owner, size), F32),
            vmem((pair_rows, depth), BF),
            vmem((nx, pair_rows, width), BF),
            vmem((nx, pair_rows, width), BF),
            vmem((3, pair_rows, width), BF),
            vmem((2, pair_rows // 2, width), BF),
            vmem((2, pair_rows, width), BF),
            dma((NC, 4)), dma((NC, 4)),
            dma((3,)), dma((3,)),
            dma((NC, 2, near)), dma((NC, 2, near)),
            dma((2, near)), dma((2, near)),
            dma((4,)), dma((4,)),
            dma((nx,)), dma((nx,)),
            dma((4,)), dma((4,)),
            dma((2,)),
        ],
        compiler_params=pltpu.CompilerParams(collective_id=0, has_side_effects=True),
    )(tiles, code, ladder_ints.T, cycle_amps, ints)


def solution(mesh):
    in_specs = (
        P(("occ", "vir"), None, None),
        P(("occ", "vir"), None),
        P(("occ", "vir")),
        P(("occ", "vir")),
        P("vir", "occ"),
        P("occ", "vir"),
        P("vir", None),
    )
    return jax.shard_map(
        functools.partial(body, mesh.shape["occ"], mesh.shape["vir"]),
        mesh=mesh, in_specs=in_specs, out_specs=P("occ", "vir"), check_vma=False,
    )
```

time: 277 us -> 123 us (0.44)
  the two profiles are of different devices: /device:TPU:8 before, /device:TPU:2 now
where the time goes in v1:
time: 123 us
  Pallas kernels  115 us (93%)
  local copies, waits for them, and re-layouts  7.52 us (6%)
    pallas_call x1, Pallas kernels, body(): pl.pallas_call(kernel, out_shape=jax.ShapeDtypeStruct((pair_rows, width),...  115 us
    unnamed x10, local copies, waits for them, and re-layouts  3.65 us

profile of v1, /device:TPU:2, one launch (start us, length us, event | category | flops | bytes accessed | tf_op | source)
XLA Modules:
  0.0 123.1 jit_solution(17941499851344924979)
XLA Ops:
  0.0 0.0 copy-start.1
  0.0 0.0 copy-start.2
  0.0 0.0 copy-start.3
  0.0 0.6 copy-done.1
  0.7 0.0 copy-done.2
  0.7 0.0 copy-done.3
  0.7 0.1 add_convert_fusion
  0.8 0.1 convert_element_type.8
  0.9 0.1 convert_element_type.9
  1.0 0.6 tile.9.code_ref
  1.6 0.0 copy-start
  1.6 1.4 %copy.10 = bf16[128,2048]{0,1:T(8,128)(2,1)S(1)} copy(bf16[128,2048]{1,0:T(8,128)(2,1)} %param.13) | data formatting | bytes 1048576 | tf_op args[6]
  3.0 1.0 copy.11
  4.0 0.0 copy-done
  4.0 2.0 %copy.9 = bf16[32,2,64,128]{3,1,0,2:T(2,128)(2,1)} copy(bf16[32,2,64,128]{3,2,1,0:T(8,128)(2,1)S(1)} %bitcast.16) | data formatting | bytes 2097152 | tf_op jit(solution)/shard_map/reshape | solution.py:341
  6.1 115.5 %shard_map.73 = bf16[256,256]{1,0:T(8,128)(2,1)} custom-call(bf16[64,64,128]{2,1,0:T(8,128)(2,1)} %bitcast.13, f32[8,128]{1,0:T(8,128)} %tile.9.code_ref, bf16[32,512]{1,0:T(8,128)(2,1)} %bitcast.17, bf16[256,128]{1,0:T(8,128)(2,1)} %camp_ref.1, bf16[8,128,256]{2,1,0:T(8,128)(2,1)} %bitcast.14), custom_call_target="tpu_custom_call" | custom-call | tf_op jit(solution)/shard_map/pallas_call | solution.py:348
  121.5 1.6 %copy.13 = bf16[256,256]{1,0:T(8,128)(2,1)} copy(bf16[256,256]{1,0:T(8,128)(2,1)} %shard_map.73) | data formatting | bytes 262144
  (2 shorter events, 0.0 us)
Async XLA Ops:
  0.0 0.7 copy-start.1
  0.0 0.7 copy-start.2
  0.0 0.7 copy-start.3
  1.6 2.4 %copy-start = (bf16[32,128,128]{2,1,0:T(8,128)(2,1)S(1)}, bf16[32,128,128]{2,1,0:T(8,128)(2,1)}, u32[]{:S(2)}) copy-start(bf16[32,128,128]{2,1,0:T(8,128)(2,1)} %param.7) | copy-start | bytes 3145732

commit v2 on v1

--- a/solution.py
+++ b/solution.py
@@ -10,7 +10,10 @@
 MESH = pl.DeviceIdType.MESH
 NY = 4
 NC = 4
-LAG = 2
+LAD_TICK = 9
+EARLY = 5
+PASS = (0, 0, 2, 3)
+BEGIN = (0, 3, 4, 5)
 BF = jnp.bfloat16
 F32 = jnp.float32
 
@@ -123,9 +126,8 @@
 
     for d in (1, 2, 3):
         code_out(d).start()
-    for c in (0, 1):
-        for d in (0, 1):
-            own_y(c, d).start()
+    for d in (0, 1):
+        own_y(0, d).start()
     mine_t2 = pltpu.make_async_copy(t2_ref, gath.at[:, y], local.at[0])
     mine_lad = pltpu.make_async_copy(lad_ref, lgat.at[y, z], local.at[1])
     mine_t2.start()
@@ -135,9 +137,10 @@
         for d in (0, 1):
             own_y_in(c, d).wait_recv()
             fwd_y(c, d).start()
-        if c + 2 < NC:
-            for d in (0, 1):
-                own_y(c + 2, d).start()
+        for n in (1, 2) if c == 0 else (c + 2,):
+            if n < NC:
+                for d in (0, 1):
+                    own_y(n, d).start()
 
     def lad_step(s):
         for d in (0, 1):
@@ -148,14 +151,19 @@
 
     lad_step(0)
 
+    width = part.shape[2]
+
     @pl.loop(0, part.shape[0])
     def _(j):
-        part[j] = jnp.dot(camp_ref[...], cint_ref[j], preferred_element_type=F32)
+        part[j] = jnp.dot(
+            camp_ref[...], cint_ref[:, pl.ds(pl.multiple_of(j * width, width), width)],
+            preferred_element_type=F32,
+        )
 
     for s in (1, 2):
         lad_step(s)
     stage_a(0)
-    for s in range(3, steps[0] + 1):
+    for s in range(3, EARLY):
         lad_step(s)
     mine_t2.wait()
     mine_lad.wait()
@@ -178,11 +186,17 @@
 
         @pl.loop(0, cr // 4)
         def _(i):
-            for u in range(4):
+            size = gath.shape[3]
+            for u in (0, 2):
                 r = c * cr + i * 4 + u
-                tiles = gath[r].reshape(NY * per_y, gath.shape[3])
-                got = jnp.dot(sel[...], tiles, preferred_element_type=F32)
-                ysum[:, r] = got.astype(BF).reshape(nz, dests // nz, gath.shape[3])
+                tiles = jnp.concatenate(
+                    [gath[r + e].reshape(NY * per_y, size) for e in (0, 1)], axis=1
+                )
+                got = jnp.dot(sel[...], tiles, preferred_element_type=F32).astype(BF)
+                for e in (0, 1):
+                    ysum[:, r + e] = got[:, e * size:(e + 1) * size].reshape(
+                        nz, dests // nz, size
+                    )
 
         for d in (0, 1):
             z_copy(c, d, 0).start()
@@ -207,18 +221,15 @@
 
     last = nz // 2
 
-    @pl.loop(0, LAG * (NC - 1) + last + 1)
+    @pl.loop(0, BEGIN[-1] + last + 1)
     def _(tick):
         for c in range(NC):
-            s = tick - LAG * c
+            s = tick - BEGIN[c]
             if c > 0:
 
-                @pl.when(s == -1)
+                @pl.when(tick == PASS[c])
                 def _():
                     stage_a(c)
-                    if c == NC - 1:
-                        for d in (0, 1):
-                            lad_y(d, 0).start()
 
             @pl.when(s == 0)
             def _():
@@ -232,13 +243,20 @@
             def _():
                 z_last(c)
 
-            if c == NC - 1:
-
-                @pl.when(s == 3)
-                def _():
+        for n in range(EARLY, steps[0] + 1):
+
+            @pl.when(tick == n - EARLY)
+            def _():
+                lad_step(n)
+                if n == steps[0]:
                     for d in (0, 1):
-                        lad_y(d, 2 * d - 1).wait_recv()
-                        lad_fwd(d, 2 * d - 1).start()
+                        lad_y(d, 0).start()
+
+        @pl.when(tick == LAD_TICK)
+        def _():
+            for d in (0, 1):
+                lad_y(d, 2 * d - 1).wait_recv()
+                lad_fwd(d, 2 * d - 1).start()
 
     for d in (0, 1):
         lad_fwd(d, 2).wait_recv()
@@ -342,7 +360,6 @@
     code = tile_owner[:, 0] * combos + tile_block * cds + tile_cd
     code = (code[:, None] * 2 + jnp.arange(2, dtype=jnp.int32)[None, :]).reshape(1, per_y)
     code = jnp.tile(code, (8, 128 // per_y)).astype(F32)
-    ints = cycle_ints.reshape(ranks, n_vir, width).transpose(1, 0, 2)
     vmem, dma = pltpu.VMEM, pltpu.SemaphoreType.DMA
     near = nz // 2
     return pl.pallas_call(
@@ -375,7 +392,7 @@
             dma((2,)),
         ],
         compiler_params=pltpu.CompilerParams(collective_id=0, has_side_effects=True),
-    )(tiles, code, ladder_ints.T, cycle_amps, ints)
+    )(tiles, code, ladder_ints.T, cycle_amps, cycle_ints)
 
 
 def solution(mesh):

time: 123 us -> 108 us (0.88)
  the two profiles are of different devices: /device:TPU:2 before, /device:TPU:40 now
where the time goes in v2:
time: 108 us
  Pallas kernels  102 us (94%)
  local copies, waits for them, and re-layouts  6.32 us (6%)
    pallas_call x1, Pallas kernels, body(): pl.pallas_call(kernel, out_shape=jax.ShapeDtypeStruct((pair_rows, width),...  102 us
    reshape x1, local copies, waits for them, and re-layouts, body(): t2_tiles.reshape(count, 2, rows, size).transpose(2, 0, 1, 3)  3.28 us
    unnamed x7, local copies, waits for them, and re-layouts  2.25 us

profile of v2, /device:TPU:40, one launch (start us, length us, event | category | flops | bytes accessed | tf_op | source)
XLA Modules:
  0.0 108.3 jit_solution(16847330033968398596)
XLA Ops:
  0.0 0.0 copy-start
  0.0 0.0 copy-start.1
  0.0 0.0 copy-start.2
  0.0 0.6 copy-done
  0.7 0.0 copy-done.1
  0.7 0.0 copy-done.2
  0.7 0.1 add_convert_fusion
  0.8 0.1 convert_element_type.8
  0.9 0.1 convert_element_type.9
  1.0 0.6 tile.9.code_ref
  1.6 3.3 %copy.9 = bf16[32,2,64,128]{3,1,0,2:T(2,128)(2,1)} copy(bf16[32,2,64,128]{3,2,1,0:T(8,128)(2,1)} %bitcast.12) | data formatting | bytes 2097152 | tf_op jit(solution)/shard_map/reshape | solution.py:359
  4.8 101.9 %shard_map.73 = bf16[256,256]{1,0:T(8,128)(2,1)} custom-call(bf16[64,64,128]{2,1,0:T(8,128)(2,1)} %bitcast.11, f32[8,128]{1,0:T(8,128)} %tile.9.code_ref, bf16[32,512]{1,0:T(8,128)(2,1)} %bitcast.13, bf16[256,128]{1,0:T(8,128)(2,1)} %camp_ref.1, bf16[128,2048]{1,0:T(8,128)(2,1)} %cint_ref.1), custom_call_target="tpu_custom_call" | custom-call | tf_op jit(solution)/shard_map/pallas_call | solution.py:365
  106.7 1.6 %copy.11 = bf16[256,256]{1,0:T(8,128)(2,1)} copy(bf16[256,256]{1,0:T(8,128)(2,1)} %shard_map.73) | data formatting | bytes 262144
  (2 shorter events, 0.0 us)
Async XLA Ops:
  0.0 0.7 copy-start
  0.0 0.7 copy-start.1
  0.0 0.7 copy-start.2

commit v3 on v2

--- a/solution.py
+++ b/solution.py
@@ -10,6 +10,7 @@
 MESH = pl.DeviceIdType.MESH
 NY = 4
 NC = 4
+SHARE = (5, 4, 4, 3)
 LAD_TICK = 9
 EARLY = 5
 PASS = (0, 0, 2, 3)
@@ -25,8 +26,8 @@
 ):
     nz = lgat.shape[1]
     rows = t2_ref.shape[0]
-    cr = rows // NC
-    half = cr // 2
+    sizes = [rows * n // 16 for n in SHARE]
+    starts = [sum(sizes[:c]) for c in range(NC)]
     nx = pout.shape[0]
     occ, vir = lax.axis_index("occ"), lax.axis_index("vir")
     y, z = occ // nz, occ % nz
@@ -59,29 +60,30 @@
         )
 
     def chunk(c):
-        return pl.ds(c * cr, cr)
+        return pl.ds(starts[c], sizes[c])
 
     def own_y(c, d):
         return remote(
-            t2_ref.at[chunk(c)], gath.at[chunk(c), y], ysend.at[c, d], yrecv.at[c, d],
+            t2_ref.at[chunk(c)], gath.at[y, chunk(c)], ysend.at[c, d], yrecv.at[c, d],
             to_y(1 - 2 * d),
         )
 
     def own_y_in(c, d):
         return remote(
-            t2_ref.at[chunk(c)], gath.at[chunk(c), at_y(2 * d - 1)], ysend.at[c, d],
+            t2_ref.at[chunk(c)], gath.at[at_y(2 * d - 1), chunk(c)], ysend.at[c, d],
             yrecv.at[c, d], to_y(1 - 2 * d),
         )
 
     def piece(c, d):
-        return pl.ds(c * cr + d * half, half)
+        half = sizes[c] // 2
+        return pl.ds(starts[c] + d * half, half)
 
     def fwd_y(c, d):
-        block = gath.at[piece(c, d), at_y(2 * d - 1)]
+        block = gath.at[at_y(2 * d - 1), piece(c, d)]
         return remote(block, block, ysend.at[c, 2 + d], yrecv.at[c, 2 + d], to_y(1 - 2 * d))
 
     def fwd_y_in(c, d):
-        block = gath.at[piece(c, d), at_y(2)]
+        block = gath.at[at_y(2), piece(c, d)]
         return remote(block, block, ysend.at[c, 2 + d], yrecv.at[c, 2 + d], to_y(1 - 2 * d))
 
     def code_out(d):
@@ -128,9 +130,7 @@
         code_out(d).start()
     for d in (0, 1):
         own_y(0, d).start()
-    mine_t2 = pltpu.make_async_copy(t2_ref, gath.at[:, y], local.at[0])
-    mine_lad = pltpu.make_async_copy(lad_ref, lgat.at[y, z], local.at[1])
-    mine_t2.start()
+    mine_lad = pltpu.make_async_copy(lad_ref, lgat.at[y, z], local.at[0])
     mine_lad.start()
 
     def stage_a(c):
@@ -153,6 +153,10 @@
 
     width = part.shape[2]
 
+    @pl.loop(0, rows)
+    def _(r):
+        gath[y, r] = t2_ref[r]
+
     @pl.loop(0, part.shape[0])
     def _(j):
         part[j] = jnp.dot(
@@ -165,7 +169,6 @@
     stage_a(0)
     for s in range(3, EARLY):
         lad_step(s)
-    mine_t2.wait()
     mine_lad.wait()
 
     codes[y] = code_ref[...]
@@ -184,13 +187,17 @@
         for d in (0, 1):
             fwd_y_in(c, d).wait_recv()
 
-        @pl.loop(0, cr // 4)
+        @pl.loop(0, sizes[c] // 4)
         def _(i):
             size = gath.shape[3]
             for u in (0, 2):
-                r = c * cr + i * 4 + u
+                r = starts[c] + i * 4 + u
                 tiles = jnp.concatenate(
-                    [gath[r + e].reshape(NY * per_y, size) for e in (0, 1)], axis=1
+                    [
+                        jnp.concatenate([gath[n, r + e] for n in range(NY)], axis=0)
+                        for e in (0, 1)
+                    ],
+                    axis=1,
                 )
                 got = jnp.dot(sel[...], tiles, preferred_element_type=F32).astype(BF)
                 for e in (0, 1):
@@ -216,8 +223,10 @@
         for d in (0, 1):
             z_copy(c, d, arm(c, d) - 1).wait_recv()
             total = total + zin[d, arm(c, d) - 1, chunk(c)].astype(F32)
-        depth = acc.shape[0] // NC
-        acc[pl.ds(c * depth, depth)] = total.reshape(depth, acc.shape[1])
+        per = acc.shape[0] // rows
+        acc[pl.ds(starts[c] * per, sizes[c] * per)] = total.reshape(
+            sizes[c] * per, acc.shape[1]
+        )
 
     last = nz // 2
 
@@ -368,7 +377,7 @@
         in_specs=[pl.BlockSpec(memory_space=vmem)] * 5,
         out_specs=pl.BlockSpec(memory_space=vmem),
         scratch_shapes=[
-            vmem((rows, NY, per_y, size), BF),
+            vmem((NY, rows, per_y, size), BF),
             vmem((NY, 8, 128), F32),
             vmem((nz * per_owner, NY * per_y), BF),
             vmem((nz, rows, per_owner, size), BF),
@@ -389,7 +398,7 @@
             dma((4,)), dma((4,)),
             dma((nx,)), dma((nx,)),
             dma((4,)), dma((4,)),
-            dma((2,)),
+            dma((1,)),
         ],
         compiler_params=pltpu.CompilerParams(collective_id=0, has_side_effects=True),
     )(tiles, code, ladder_ints.T, cycle_amps, cycle_ints)

time: 108 us -> 108 us (level)
  the two profiles are of different devices: /device:TPU:40 before, /device:TPU:2 now
where the time goes in v3:
time: 108 us
  Pallas kernels  101 us (94%)
  local copies, waits for them, and re-layouts  6.32 us (6%)
    pallas_call x1, Pallas kernels, body(): pl.pallas_call(kernel, out_shape=jax.ShapeDtypeStruct((pair_rows, width),...  101 us
    reshape x1, local copies, waits for them, and re-layouts, body(): t2_tiles.reshape(count, 2, rows, size).transpose(2, 0, 1, 3)  3.28 us
    unnamed x7, local copies, waits for them, and re-layouts  2.25 us

profile of v3, /device:TPU:2, one launch (start us, length us, event | category | flops | bytes accessed | tf_op | source)
XLA Modules:
  0.0 107.6 jit_solution(4653805361870209400)
XLA Ops:
  0.0 0.0 copy-start
  0.0 0.0 copy-start.1
  0.0 0.0 copy-start.2
  0.0 0.6 copy-done
  0.7 0.0 copy-done.1
  0.7 0.0 copy-done.2
  0.7 0.1 add_convert_fusion
  0.8 0.1 convert_element_type.8
  0.9 0.1 convert_element_type.9
  1.0 0.6 tile.9.code_ref
  1.6 3.3 %copy.9 = bf16[32,2,64,128]{3,1,0,2:T(2,128)(2,1)} copy(bf16[32,2,64,128]{3,2,1,0:T(8,128)(2,1)} %bitcast.12) | data formatting | bytes 2097152 | tf_op jit(solution)/shard_map/reshape | solution.py:368
  4.8 101.2 %shard_map.73 = bf16[256,256]{1,0:T(8,128)(2,1)} custom-call(bf16[64,64,128]{2,1,0:T(8,128)(2,1)} %bitcast.11, f32[8,128]{1,0:T(8,128)} %tile.9.code_ref, bf16[32,512]{1,0:T(8,128)(2,1)} %bitcast.13, bf16[256,128]{1,0:T(8,128)(2,1)} %camp_ref.1, bf16[128,2048]{1,0:T(8,128)(2,1)} %cint_ref.1), custom_call_target="tpu_custom_call" | custom-call | tf_op jit(solution)/shard_map/pallas_call | solution.py:374
  106.0 1.6 %copy.11 = bf16[256,256]{1,0:T(8,128)(2,1)} copy(bf16[256,256]{1,0:T(8,128)(2,1)} %shard_map.73) | data formatting | bytes 262144
  (2 shorter events, 0.0 us)
Async XLA Ops:
  0.0 0.7 copy-start
  0.0 0.7 copy-start.1
  0.0 0.7 copy-start.2
